TPU v7x, 32 devices: a whole 2x2x4 slice. The times are simulated.
32 devices in a mesh: dp: 4 (over z), tensor: 8 (over y, x, core).
Axes of the slice: x: 2, y: 2, z: 4, core: 2. Of those that a mesh axis runs over, the one named last changes fastest.
Arguments:
- activations: bfloat16 [3072, 4096], P('dp', 'tensor'), may hold values from -6 to 6
- out_grads_t: bfloat16 [5504, 3072], P('tensor', 'dp'), may hold values from -6 to 6
- in_basis: bfloat16 [4096, 4096], P(None, 'tensor'), may hold values from -0.09375 to 0.09375
- out_basis_t: bfloat16 [5504, 5504], P('tensor'), may hold values from -0.078125 to 0.078125
- query_proj: bfloat16 [4, 5504, 4096], P(None, 'tensor', 'dp'), may hold values from -6 to 6
- eigvals: float32 [5504, 4096], P('tensor', 'dp'), may hold values from 0.05 to 5
- damping: float32 [1], replicated, may hold values from 0.05 to 0.2
- lengths: int32 [24], P('dp'), may hold values from 1 to 128, 1920 in all
Outputs:
- scores: float32 [24, 4], P('dp')
Inputs may be any that keep to these rules, and one draw needn't show every extreme that they name: `lengths`: the largest token count is exactly 128.
All inputs are finite; a program needn't handle non-finite values. No bound on the sum of `lengths` on one device may be relied on, other than what follows from the above.
Results may differ from a plain program's by a relative error of at most 0.006.
Values may be sent and summed in bfloat16 or wider, within the bound.
A program may use at most 128 MiB of HBM per device.

v0:
```python
import jax
import jax.numpy as jnp
from jax import lax
from jax.sharding import PartitionSpec as P


def local(activations, out_grads_t, in_basis, out_basis_t, query_proj, eigvals, damping, lengths):
    full_act = lax.all_gather(activations, "tensor", axis=1, tiled=True)
    act_local = jnp.dot(full_act, in_basis, preferred_element_type=jnp.float32).astype(jnp.bfloat16)
    act_proj = lax.all_gather(act_local, "tensor", axis=1, tiled=True)
    token_rows = full_act.shape[0]
    width = out_basis_t.shape[0]
    grad_full = jnp.dot(
        out_basis_t,
        lax.all_gather(out_grads_t, "tensor", axis=0, tiled=True),
        preferred_element_type=jnp.float32,
    )
    seq_count = lengths.shape[0]
    seq_len = token_rows // seq_count
    position = lax.broadcasted_iota(jnp.int32, (seq_count, seq_len), 1)
    keep = (position < lengths[:, None]).astype(jnp.float32).reshape(1, token_rows)
    grad_proj = (grad_full * keep).astype(jnp.bfloat16)
    scaled = (query_proj.astype(jnp.float32) / (eigvals + damping[0])).astype(jnp.bfloat16)
    query_count = query_proj.shape[0]
    mixed = jnp.einsum(
        "td,qjd->qjt",
        act_proj,
        lax.all_gather(scaled, "dp", axis=2, tiled=True),
        preferred_element_type=jnp.float32,
    )
    weighted = mixed * grad_proj.astype(jnp.float32)[None, :, :]
    partial_value = jnp.sum(weighted.reshape(query_count, width, seq_count, seq_len), axis=(1, 3)).T
    totals = lax.psum(partial_value, "tensor")
    norm_factor = (act_proj.shape[1] * out_basis_t.shape[1] * seq_len) ** (-0.5)
    return totals * norm_factor


def solution(mesh):
    placed = (
        P("dp", "tensor"),
        P("tensor", "dp"),
        P(None, "tensor"),
        P("tensor", None),
        P(None, "tensor", "dp"),
        P("tensor", "dp"),
        P(),
        P("dp"),
    )
    return jax.shard_map(
        local, mesh=mesh, in_specs=placed, out_specs=P("dp", None), check_vma=False
    )
```

profile of v0, /device:TPU:0, one launch (start us, length us, event | category | flops | bytes accessed | tf_op | source)
XLA Modules:
  0.0 591.1 jit_solution(7677577895891891836)
XLA Ops:
  6.5 0.0 all-gather.7.cloned.1.call-start
  6.5 0.7 all-gather.7.cloned.1.call-update
  7.3 0.0 all-gather.11.cloned.1.call-start
  7.3 0.7 all-gather.11.cloned.1.call-update
  8.0 0.0 copy-start
  8.0 0.0 all-gather.9.cloned.1.call-start
  8.1 50.5 %all-gather.7.cloned.1.call-done = bf16[768,4096]{1,0:T(8,128)(2,1)} async-done(((bf16[768,512]{1,0:T(8,128)(2,1)}), bf16[768,4096]{1,0:T(8,128)(2,1)}) %all-gather.7.cloned.1.call-update) | async-done | bytes 6291472 | tf_op jit(solution)/shard_map/all_gather | solution.py:8
  58.5 8.3 %convolution_convert_fusion = bf16[768,512]{1,0:T(8,128)(2,1)} fusion(bf16[768,4096]{1,0:T(8,128)(2,1)} %all-gather.7.cloned.1.call-done, bf16[4096,512]{1,0:T(8,128)(2,1)} %param.10), kind=kOutput, calls=%fused_computation.7 | convolution fusion | flops 3221618688 | bytes 11272192 | tf_op jit(solution)/shard_map/dot_general | solution.py:9
  66.9 0.0 all-gather.9.cloned.1.call-update
  66.9 0.0 all-gather.5.cloned.1.call-start
  67.6 0.0 copy-done
  67.6 0.5 broadcast_add_fusion
  68.1 0.0 copy-start.1
  68.1 7.5 %divide_convert_fusion = bf16[4,688,1024]{2,1,0:T(8,128)(2,1)} fusion(bf16[4,688,1024]{2,1,0:T(8,128)(2,1)} %param.12, f32[688,1024]{1,0:T(8,128)S(1)} %broadcast_add_fusion), kind=kLoop, calls=%fused_computation | loop fusion | flops 8454144 | bytes 14090240 | tf_op jit(solution)/shard_map/convert_element_type | solution.py:23
  75.6 0.0 all-gather.5.cloned.1.call-update
  75.6 0.0 copy-done.1
  75.6 0.1 convert_bitcast_fusion
  75.7 39.3 %all-gather.11.cloned.1.call-done = bf16[5504,768]{1,0:T(8,128)(2,1)} async-done(((bf16[688,768]{1,0:T(8,128)(2,1)}), bf16[5504,768]{1,0:T(8,128)(2,1)}) %all-gather.11.cloned.1.call-update) | async-done | bytes 8454160 | tf_op jit(solution)/shard_map/all_gather | solution.py:15
  115.0 10.9 %fusion.4 = f32[688,768]{1,0:T(8,128)S(1)} fusion(bf16[688,5504]{1,0:T(8,128)(2,1)} %param.11, bf16[5504,768]{1,0:T(8,128)(2,1)} %all-gather.11.cloned.1.call-done, f32[768]{0:T(1024)S(1)} %convert_bitcast_fusion), kind=kOutput, calls=%fused_computation.5 | convolution fusion | flops 5818036224 | bytes 18144256 | tf_op jit(solution)/shard_map/dot_general | solution.py:13
  125.9 37.6 %all-gather.9.cloned.1.call-done = bf16[768,4096]{1,0:T(8,128)(2,1)} async-done(((bf16[768,512]{1,0:T(8,128)(2,1)}), bf16[768,4096]{1,0:T(8,128)(2,1)}) %all-gather.9.cloned.1.call-update) | async-done | bytes 6291472 | tf_op jit(solution)/shard_map/all_gather | solution.py:10
  163.5 384.0 %all-gather.5.cloned.1.call-done = bf16[4,688,4096]{2,1,0:T(8,128)(2,1)} async-done(((bf16[4,688,1024]{2,1,0:T(8,128)(2,1)}), bf16[4,688,4096]{2,1,0:T(8,128)(2,1)}) %all-gather.5.cloned.1.call-update) | async-done | bytes 22544400 | tf_op jit(solution)/shard_map/all_gather | solution.py:28
  547.5 22.8 %multiply_reduce_fusion = f32[4,768]{1,0:T(4,128)S(1)} fusion(f32[688,768]{1,0:T(8,128)S(1)} %fusion.4, bf16[4,688,4096]{2,1,0:T(8,128)(2,1)} %all-gather.5.cloned.1.call-done, bf16[768,4096]{1,0:T(8,128)(2,1)} %all-gather.9.cloned.1.call-done), kind=kOutput, calls=%fused_computation.1 | convolution fusion | flops 17318309888 | bytes 30961664 | tf_op jit(solution)/shard_map/td,qjd->qjt/dot_general | solution.py:25
  570.3 0.1 reduce_sum.18
  570.4 13.6 %psum.7 = f32[6,4]{0,1:T(4,128)S(1)} all-reduce(f32[6,4]{0,1:T(4,128)S(1)} %bitcast.15), channel_id=1, replica_groups=mesh['dp'=4,'tensor'=8] {'tensor'}, use_global_device_ids=true, to_apply=%region_2.3 | all-reduce | flops 24 | bytes 192 | tf_op jit(solution)/shard_map/psum | solution.py:33
  584.0 0.6 broadcast_multiply_fusion
  (1 shorter events, 0.0 us)
Async XLA Ops:
  6.5 52.0 %all-gather.7.cloned.1.call-start = ((), (), s32[]{:S(2)}) async-start(), calls=%async_computation.1 | async-start | bytes 7077888 | tf_op jit(solution)/shard_map/all_gather | solution.py:8
  7.3 107.7 %all-gather.11.cloned.1.call-start = ((), (), s32[]{:S(2)}) async-start(), calls=%async_computation.3 | async-start | bytes 9510912 | tf_op jit(solution)/shard_map/all_gather | solution.py:15
  8.0 59.6 %copy-start = (f32[688,1024]{1,0:T(8,128)S(1)}, f32[688,1024]{1,0:T(8,128)}, u32[]{:S(2)}) copy-start(f32[688,1024]{1,0:T(8,128)} %param.13) | copy-start | bytes 8454148
  8.0 155.5 %all-gather.9.cloned.1.call-start = ((), (), s32[]{:S(2)}) async-start(), calls=%async_computation.2 | async-start | bytes 7077888 | tf_op jit(solution)/shard_map/all_gather | solution.py:10
  66.9 480.6 %all-gather.5.cloned.1.call-start = ((), (), s32[]{:S(2)}) async-start(), calls=%async_computation | async-start | bytes 28180480 | tf_op jit(solution)/shard_map/all_gather | solution.py:28
  68.1 7.5 %copy-start.1 = (s32[6]{0:T(128)S(1)}, s32[6]{0:T(128)}, u32[]{:S(2)}) copy-start(s32[6]{0:T(128)} %param.15) | copy-start | bytes 76
Sparse Core Ops, SparseCore 0:
  9.2 49.2 all-gather.6
  60.4 54.5 all-gather.10
  116.9 46.5 all-gather.8
  164.9 382.4 all-gather.4
where the time goes:
time: 591 us
  waiting for transfers between devices  513 us (87%)
  matrix products  42 us (7%)
  between operations  13.8 us (2%)
  blocking collectives  13.6 us (2%)
  other arithmetic  8.66 us (1%)
    all_gather x1, waiting for transfers between devices, local(): lax.all_gather(scaled, 'dp', axis=2, tiled=True)  384 us
    all_gather x1, waiting for transfers between devices, local(): full_act = lax.all_gather(activations, 'tensor', axis=1, tiled=True)  50.5 us
    all_gather x1, waiting for transfers between devices, local(): lax.all_gather(out_grads_t, 'tensor', axis=0, tiled=True)  39.3 us
    all_gather x1, waiting for transfers between devices, local(): act_proj = lax.all_gather(act_local, 'tensor', axis=1, tiled=True)  37.6 us
    dot_general x1, matrix products, local(): jnp.einsum('td,qjd->qjt', act_proj, lax.all_gather(scaled, 'dp', axis=2,...  22.8 us
    psum x1, blocking collectives, local(): totals = lax.psum(partial_value, 'tensor')  13.6 us
  transfers between devices with their start and end apart: 4, of which 4 were waited for; matrix products, arithmetic and copies ran while one was open for 5% of the time, Pallas kernels for 0%

commit v1 on v0

--- a/solution.py
+++ b/solution.py
@@ -7,7 +7,14 @@
 def local(activations, out_grads_t, in_basis, out_basis_t, query_proj, eigvals, damping, lengths):
     full_act = lax.all_gather(activations, "tensor", axis=1, tiled=True)
     act_local = jnp.dot(full_act, in_basis, preferred_element_type=jnp.float32).astype(jnp.bfloat16)
-    act_proj = lax.all_gather(act_local, "tensor", axis=1, tiled=True)
+    ring = [act_local]
+    for hop in range(7):
+        ring.append(lax.ppermute(ring[-1], "tensor", [(dev, (dev + 1) % 8) for dev in range(8)]))
+    act_proj = jnp.roll(
+        jnp.concatenate(ring[::-1], axis=1),
+        (lax.axis_index("tensor") + 1) * ring[0].shape[1],
+        axis=1,
+    )
     token_rows = full_act.shape[0]
     width = out_basis_t.shape[0]
     grad_full = jnp.dot(

time: 591 us -> 558 us (0.944)
  waiting for transfers between devices: 513 us -> 455 us
  local copies, waits for them, and re-layouts: 0.02 us -> 22.9 us
    ppermute x0 -> x7, waiting for transfers between devices: none -> 105 us  [local(): lax.ppermute(ring[-1], 'tensor', [(dev, (dev + 1) % 8) for dev in range(8)])]
    all_gather x1, waiting for transfers between devices: 384 us -> 308 us  [local(): lax.all_gather(scaled, 'dp', axis=2, tiled=True)]
    all_gather x1, waiting for transfers between devices: 39.3 us -> 0.01 us  [local(): lax.all_gather(out_grads_t, 'tensor', axis=0, tiled=True)]
    all_gather x1 -> x0, waiting for transfers between devices: 37.6 us -> none  [local(): act_proj = lax.all_gather(act_local, 'tensor', axis=1, tiled=True)]
    unnamed x4 -> x21, local copies, waits for them, and re-layouts: 0.01 us -> 22 us
    all_gather x1, waiting for transfers between devices: 50.5 us -> 40.6 us  [local(): full_act = lax.all_gather(activations, 'tensor', axis=1, tiled=True)]
  transfers between devices with their start and end apart: 4 -> 10, of which waited for: 4 -> 9; matrix products, arithmetic and copies ran while one was open for 5% -> 9% of each run, Pallas kernels for 0% -> 0%
where the time goes in v1:
time: 558 us
  waiting for transfers between devices  455 us (82%)
  matrix products  42.6 us (8%)
  local copies, waits for them, and re-layouts  22.9 us (4%)
  between operations  13.8 us (2%)
  blocking collectives  13.6 us (2%)
  other arithmetic  9.93 us (2%)
    all_gather x1, waiting for transfers between devices, local(): lax.all_gather(scaled, 'dp', axis=2, tiled=True)  308 us
    ppermute x7, waiting for transfers between devices, local(): lax.ppermute(ring[-1], 'tensor', [(dev, (dev + 1) % 8) for dev in range(8)])  105 us
    all_gather x1, waiting for transfers between devices, local(): full_act = lax.all_gather(activations, 'tensor', axis=1, tiled=True)  40.6 us
    dot_general x1, matrix products, local(): jnp.einsum('td,qjd->qjt', act_proj, lax.all_gather(scaled, 'dp', axis=2,...  23 us
    unnamed x21, local copies, waits for them, and re-layouts  22 us
    psum x1, blocking collectives, local(): totals = lax.psum(partial_value, 'tensor')  13.6 us
    dot_general x1, matrix products, local(): jnp.dot(out_basis_t, lax.all_gather(out_grads_t, 'tensor', axis=0, tiled=...  12.1 us
  transfers between devices with their start and end apart: 10, of which 9 were waited for; matrix products, arithmetic and copies ran while one was open for 9% of the time, Pallas kernels for 0%

profile of v1, /device:TPU:0, one launch (start us, length us, event | category | flops | bytes accessed | tf_op | source)
XLA Modules:
  0.0 557.8 jit_solution(12888190285743024304)
XLA Ops:
  6.5 0.0 all-gather.6.cloned.1.call-start
  6.5 0.7 all-gather.6.cloned.1.call-update
  7.3 0.0 all-gather.8.cloned.1.call-start
  7.3 0.7 all-gather.8.cloned.1.call-update
  8.0 0.0 all-gather.4.cloned.1.call-start
  8.7 2.1 broadcast_add_fusion
  10.8 7.1 %divide_convert_fusion = bf16[4,688,1024]{2,1,0:T(8,128)(2,1)} fusion(bf16[4,688,1024]{2,1,0:T(8,128)(2,1)} %param.12, f32[688,1024]{1,0:T(8,128)S(1)} %broadcast_add_fusion), kind=kLoop, calls=%fused_computation | loop fusion | flops 8454144 | bytes 14090240 | tf_op jit(solution)/shard_map/convert_element_type | solution.py:30
  17.9 0.0 all-gather.4.cloned.1.call-update
  17.9 0.0 copy-start.2
  17.9 40.6 %all-gather.6.cloned.1.call-done = bf16[768,4096]{1,0:T(8,128)(2,1)} async-done(((bf16[768,512]{1,0:T(8,128)(2,1)}), bf16[768,4096]{1,0:T(8,128)(2,1)}) %all-gather.6.cloned.1.call-update) | async-done | bytes 6291472 | tf_op jit(solution)/shard_map/all_gather | solution.py:8
  58.5 7.5 %convolution_convert_fusion = bf16[768,512]{0,1:T(8,128)(2,1)S(1)} fusion(bf16[768,4096]{1,0:T(8,128)(2,1)} %all-gather.6.cloned.1.call-done, bf16[4096,512]{1,0:T(8,128)(2,1)} %param.10), kind=kOutput, calls=%fused_computation.8 | convolution fusion | flops 3221618688 | bytes 11272192 | tf_op jit(solution)/shard_map/dot_general | solution.py:9
  66.0 0.3 collective-permute-start
  66.3 23.4 %collective-permute-done = bf16[768,512]{0,1:T(8,128)(2,1)S(1)} collective-permute-done((bf16[768,512]{0,1:T(8,128)(2,1)S(1)}, bf16[768,512]{0,1:T(8,128)(2,1)S(1)}, u32[]{:S(2)}, u32[]{:S(2)}) %collective-permute-start) | collective-permute-done | bytes 786464 | tf_op jit(solution)/shard_map/ppermute | solution.py:12
  89.7 0.0 collective-permute-start.1
  89.7 23.1 %collective-permute-done.1 = bf16[768,512]{0,1:T(8,128)(2,1)S(1)} collective-permute-done((bf16[768,512]{0,1:T(8,128)(2,1)S(1)}, bf16[768,512]{0,1:T(8,128)(2,1)S(1)}, u32[]{:S(2)}, u32[]{:S(2)}) %collective-permute-start.1) | collective-permute-done | bytes 786464 | tf_op jit(solution)/shard_map/ppermute | solution.py:12
  112.8 0.0 collective-permute-start.2
  112.8 20.3 %collective-permute-done.2 = bf16[768,512]{0,1:T(8,128)(2,1)S(1)} collective-permute-done((bf16[768,512]{0,1:T(8,128)(2,1)S(1)}, bf16[768,512]{0,1:T(8,128)(2,1)S(1)}, u32[]{:S(2)}, u32[]{:S(2)}) %collective-permute-start.2) | collective-permute-done | bytes 786464 | tf_op jit(solution)/shard_map/ppermute | solution.py:12
  133.1 0.0 collective-permute-start.3
  133.1 12.3 %collective-permute-done.3 = bf16[768,512]{0,1:T(8,128)(2,1)S(1)} collective-permute-done((bf16[768,512]{0,1:T(8,128)(2,1)S(1)}, bf16[768,512]{0,1:T(8,128)(2,1)S(1)}, u32[]{:S(2)}, u32[]{:S(2)}) %collective-permute-start.3) | collective-permute-done | bytes 786464 | tf_op jit(solution)/shard_map/ppermute | solution.py:12
  145.4 0.0 copy-start
  145.4 0.9 copy-done
  146.3 0.0 collective-permute-start.4
  146.3 12.4 %collective-permute-done.4 = bf16[768,512]{0,1:T(8,128)(2,1)} collective-permute-done((bf16[768,512]{0,1:T(8,128)(2,1)S(1)}, bf16[768,512]{0,1:T(8,128)(2,1)}, u32[]{:S(2)}, u32[]{:S(2)}) %collective-permute-start.4) | collective-permute-done | bytes 786464 | tf_op jit(solution)/shard_map/ppermute | solution.py:12
  158.7 0.0 collective-permute-start.5
  158.7 0.0 copy-done.2
  158.7 0.1 convert_bitcast_fusion
  158.8 12.6 %collective-permute-done.5 = bf16[768,512]{0,1:T(8,128)(2,1)} collective-permute-done((bf16[768,512]{0,1:T(8,128)(2,1)}, bf16[768,512]{0,1:T(8,128)(2,1)}, u32[]{:S(2)}, u32[]{:S(2)}) %collective-permute-start.5) | collective-permute-done | bytes 786464 | tf_op jit(solution)/shard_map/ppermute | solution.py:12
  171.3 0.0 collective-permute-start.6
  171.4 0.0 all-gather.8.cloned.1.call-done
  171.4 0.0 copy-start.1
  171.4 12.1 %fusion.5 = f32[688,768]{1,0:T(8,128)} fusion(bf16[688,5504]{1,0:T(8,128)(2,1)} %param.11, bf16[5504,768]{1,0:T(8,128)(2,1)} %all-gather.8.cloned.1.call-done, f32[768]{0:T(1024)S(1)} %convert_bitcast_fusion), kind=kOutput, calls=%fused_computation.6 | convolution fusion | flops 5818036224 | bytes 18144256 | tf_op jit(solution)/shard_map/dot_general | solution.py:20
  183.4 0.6 collective-permute-done.6
  184.0 2.1 constant_dynamic-update-slice_fusion.15
  186.1 2.1 constant_dynamic-update-slice_fusion.14
  188.2 2.1 constant_dynamic-update-slice_fusion.13
  190.2 0.0 copy-done.1
  190.2 1.0 constant_dynamic-update-slice_fusion.12
  191.2 0.9 constant_dynamic-update-slice_fusion.11
  192.1 0.9 constant_dynamic-update-slice_fusion.10
  193.1 0.9 constant_dynamic-update-slice_fusion.9
  194.0 0.9 constant_dynamic-update-slice_fusion.8
  194.9 2.1 constant_dynamic-update-slice_fusion.7
  197.0 2.1 constant_dynamic-update-slice_fusion.6
  199.1 2.1 constant_dynamic-update-slice_fusion.5
  201.2 0.9 constant_dynamic-update-slice_fusion.4
  202.1 1.0 constant_dynamic-update-slice_fusion.3
  203.1 0.9 constant_dynamic-update-slice_fusion.2
  204.1 1.0 constant_dynamic-update-slice_fusion.1
  205.0 0.9 constant_dynamic-update-slice_fusion
  206.0 307.9 %all-gather.4.cloned.1.call-done = bf16[4,688,4096]{2,1,0:T(8,128)(2,1)} async-done(((bf16[4,688,1024]{2,1,0:T(8,128)(2,1)}), bf16[4,688,4096]{2,1,0:T(8,128)(2,1)}) %all-gather.4.cloned.1.call-update) | async-done | bytes 22544400 | tf_op jit(solution)/shard_map/all_gather | solution.py:35
  513.9 23.0 %multiply_reduce_fusion = f32[4,768]{1,0:T(4,128)S(1)} fusion(f32[688,768]{1,0:T(8,128)} %fusion.5, bf16[4,688,4096]{2,1,0:T(8,128)(2,1)} %all-gather.4.cloned.1.call-done, bf16[768,8192]{0,1:T(8,128)(2,1)} %constant_dynamic-update-slice_fusion, s32[]{:T(128)S(6)} %select_n.14), kind=kOutput, calls=%fused_computation.1 | convolution fusion | flops 17318309888 | bytes 30961668 | tf_op jit(solution)/shard_map/td,qjd->qjt/dot_general | solution.py:32
  537.0 0.1 reduce_sum.18
  537.1 13.6 %psum.7 = f32[6,4]{0,1:T(4,128)S(1)} all-reduce(f32[6,4]{0,1:T(4,128)S(1)} %bitcast.15), channel_id=1, replica_groups=mesh['dp'=4,'tensor'=8] {'tensor'}, use_global_device_ids=true, to_apply=%region_2.3 | all-reduce | flops 24 | bytes 192 | tf_op jit(solution)/shard_map/psum | solution.py:40
  550.7 0.6 broadcast_multiply_fusion
  (1 shorter events, 0.0 us)
Async XLA Ops:
  6.5 52.0 %all-gather.6.cloned.1.call-start = ((), (), s32[]{:S(2)}) async-start(), calls=%async_computation.1 | async-start | bytes 7077888 | tf_op jit(solution)/shard_map/all_gather | solution.py:8
  7.3 164.1 %all-gather.8.cloned.1.call-start = ((), (), s32[]{:S(2)}) async-start(), calls=%async_computation.2 | async-start | bytes 9510912 | tf_op jit(solution)/shard_map/all_gather | solution.py:22
  8.0 505.9 %all-gather.4.cloned.1.call-start = ((), (), s32[]{:S(2)}) async-start(), calls=%async_computation | async-start | bytes 28180480 | tf_op jit(solution)/shard_map/all_gather | solution.py:35
  17.9 140.8 %copy-start.2 = (s32[6]{0:T(128)S(1)}, s32[6]{0:T(128)}, u32[]{:S(2)}) copy-start(s32[6]{0:T(128)} %param.15) | copy-start | bytes 76
  66.0 23.7 %collective-permute-start = (bf16[768,512]{0,1:T(8,128)(2,1)S(1)}, bf16[768,512]{0,1:T(8,128)(2,1)S(1)}, u32[]{:S(2)}, u32[]{:S(2)}) collective-permute-start(bf16[768,512]{0,1:T(8,128)(2,1)S(1)} %convolution_convert_fusion), channel_id=1, source_target_pairs={{0,1},{1,2},{2,3},{3,4},{4,5},{5,6},{6,7},{7,0},{8,9},{9,10},{10,1... | collective-permute-start | bytes 2359304 | tf_op jit(solution)/shard_map/ppermute | solution.py:12
  89.7 23.1 %collective-permute-start.1 = (bf16[768,512]{0,1:T(8,128)(2,1)S(1)}, bf16[768,512]{0,1:T(8,128)(2,1)S(1)}, u32[]{:S(2)}, u32[]{:S(2)}) collective-permute-start(bf16[768,512]{0,1:T(8,128)(2,1)S(1)} %collective-permute-done), channel_id=1, source_target_pairs={{0,1},{1,2},{2,3},{3,4},{4,5},{5,6},{6,7},{7,0},{8,9},{9,10},{10,1... | collective-permute-start | bytes 2359304 | tf_op jit(solution)/shard_map/ppermute | solution.py:12
  112.8 20.3 %collective-permute-start.2 = (bf16[768,512]{0,1:T(8,128)(2,1)S(1)}, bf16[768,512]{0,1:T(8,128)(2,1)S(1)}, u32[]{:S(2)}, u32[]{:S(2)}) collective-permute-start(bf16[768,512]{0,1:T(8,128)(2,1)S(1)} %collective-permute-done.1), channel_id=1, source_target_pairs={{0,1},{1,2},{2,3},{3,4},{4,5},{5,6},{6,7},{7,0},{8,9},{9,10},{10,1... | collective-permute-start | bytes 2359304 | tf_op jit(solution)/shard_map/ppermute | solution.py:12
  133.1 12.3 %collective-permute-start.3 = (bf16[768,512]{0,1:T(8,128)(2,1)S(1)}, bf16[768,512]{0,1:T(8,128)(2,1)S(1)}, u32[]{:S(2)}, u32[]{:S(2)}) collective-permute-start(bf16[768,512]{0,1:T(8,128)(2,1)S(1)} %collective-permute-done.2), channel_id=1, source_target_pairs={{0,1},{1,2},{2,3},{3,4},{4,5},{5,6},{6,7},{7,0},{8,9},{9,10},{10,1... | collective-permute-start | bytes 2359304 | tf_op jit(solution)/shard_map/ppermute | solution.py:12
  145.4 0.9 copy-start
  146.3 12.4 %collective-permute-start.4 = (bf16[768,512]{0,1:T(8,128)(2,1)S(1)}, bf16[768,512]{0,1:T(8,128)(2,1)}, u32[]{:S(2)}, u32[]{:S(2)}) collective-permute-start(bf16[768,512]{0,1:T(8,128)(2,1)S(1)} %collective-permute-done.3), channel_id=1, source_target_pairs={{0,1},{1,2},{2,3},{3,4},{4,5},{5,6},{6,7},{7,0},{8,9},{9,10},{10,1... | collective-permute-start | bytes 2359304 | tf_op jit(solution)/shard_map/ppermute | solution.py:12
  158.7 12.6 %collective-permute-start.5 = (bf16[768,512]{0,1:T(8,128)(2,1)}, bf16[768,512]{0,1:T(8,128)(2,1)}, u32[]{:S(2)}, u32[]{:S(2)}) collective-permute-start(bf16[768,512]{0,1:T(8,128)(2,1)} %collective-permute-done.4), channel_id=1, source_target_pairs={{0,1},{1,2},{2,3},{3,4},{4,5},{5,6},{6,7},{7,0},{8,9},{9,10},{10,1... | collective-permute-start | bytes 2359304 | tf_op jit(solution)/shard_map/ppermute | solution.py:12
  171.3 12.6 %collective-permute-start.6 = (bf16[768,512]{0,1:T(8,128)(2,1)}, bf16[768,512]{0,1:T(8,128)(2,1)}, u32[]{:S(2)}, u32[]{:S(2)}) collective-permute-start(bf16[768,512]{0,1:T(8,128)(2,1)} %collective-permute-done.5), channel_id=1, source_target_pairs={{0,1},{1,2},{2,3},{3,4},{4,5},{5,6},{6,7},{7,0},{8,9},{9,10},{10,1... | collective-permute-start | bytes 2359304 | tf_op jit(solution)/shard_map/ppermute | solution.py:12
  171.4 18.9 %copy-start.1 = (bf16[768,512]{0,1:T(8,128)(2,1)S(1)}, bf16[768,512]{0,1:T(8,128)(2,1)}, u32[]{:S(2)}) copy-start(bf16[768,512]{0,1:T(8,128)(2,1)} %copy-done) | copy-start | bytes 2359300
Sparse Core Ops, SparseCore 0:
  9.2 49.2 all-gather.5
  60.4 70.1 all-gather.7
  132.2 381.6 all-gather.3
